TPU v7x, 32 devices: a whole 2x2x4 slice. The times are simulated.
32 devices in a mesh: grp: 1, row: 32 (over z, y, x, core).
Axes of the slice: x: 2, y: 2, z: 4, core: 2. Of those that a mesh axis runs over, the one named last changes fastest.
Arguments:
- homolog_matrix: bfloat16 [64, 128, 256], P(('grp', 'row')), may hold values from -6 to 6
- alignment_mask: int32 [64, 128], P(('grp', 'row')), may hold values from 0 to 1, as said below
- pair_state_input: bfloat16 [128, 128, 128], P(('grp', 'row')), may hold values from -3 to 3
- chain_label: int32 [128], P('grp'), may hold values from 0 to 3, never falling along the last dimension, each value on 1 to 64 neighbouring positions
- residue_number_index: int32 [128], P('grp'), may hold values from 1 to 382, as said below
- relative_position_table: float32 [66, 128], replicated, may hold values from -3 to 3
- tensor_factor_coefficients: bfloat16 [256, 64], replicated, may hold values from -0.375 to 0.375
- outer_output_weight: bfloat16 [1024, 128], replicated, may hold values from -3 to 3
- scorer_entry_coefficients: bfloat16 [256, 1024], replicated, may hold values from -0.375 to 0.375
- scorer_final_coefficients: bfloat16 [256, 256], replicated, may hold values from -0.375 to 0.375
- pair_bias_weight: bfloat16 [128, 8], replicated
- triangle_input_weight: bfloat16 [128, 512], replicated, may hold values from -0.5 to 0.5
- triangle_output_gate: bfloat16 [128, 128], replicated, may hold values from -1.5 to 1.5
- triangle_output_weight: bfloat16 [128, 128], replicated, may hold values from -1.796875 to 1.796875
Outputs:
- homolog_revised: bfloat16 [64, 128, 256], P(('grp', 'row'))
- pair_state_output: bfloat16 [128, 128, 128], P(('grp', 'row'))
Inputs may be any that keep to these rules, and one draw needn't show every extreme that they name: `alignment_mask`: 1 marks a live entry of an MSA row. `chain_label`: chain ids never fall along the residues; a chain holds at most 64 residues. `residue_number_index`: residue numbers strictly increase along the residues.
All inputs are finite; a program needn't handle non-finite values.
Results may differ from a plain program's by a relative error of at most 0.03.
Values may be sent and summed in bfloat16 or wider, within the bound.
A program may use at most 128 MiB of HBM per device.

v0:
```python
import jax
import jax.numpy as jnp
from jax import lax
from jax.sharding import PartitionSpec as P

REL_MAX = 32


def layer_normalize(values):
    centre = jnp.mean(values, axis=-1, keepdims=True)
    shifted = values - centre
    spread = jnp.mean(shifted * shifted, axis=-1, keepdims=True)
    return shifted * lax.rsqrt(spread + 1e-05)


def on_device(
    homolog_matrix,
    alignment_mask,
    pair_state_input,
    chain_label,
    residue_number_index,
    relative_position_table,
    tensor_factor_coefficients,
    outer_output_weight,
    scorer_entry_coefficients,
    scorer_final_coefficients,
    pair_bias_weight,
    triangle_input_weight,
    triangle_output_gate,
    triangle_output_weight,
):
    sequence_local_rows = homolog_matrix.shape[0]
    residue_total = homolog_matrix.shape[1]
    alignment_width = homolog_matrix.shape[2]
    res_local = pair_state_input.shape[0]
    pair_width = pair_state_input.shape[2]
    opm_width = tensor_factor_coefficients.shape[1] // 2
    head_total = pair_bias_weight.shape[1]
    head_channel_width = alignment_width // head_total
    tri_width = triangle_input_weight.shape[1] // 4
    table_rows = relative_position_table.shape[0]
    row_start = lax.axis_index("row") * res_local
    contract = (((0,), (0,)), ((), ()))
    active_entry_mask = alignment_mask.astype(jnp.float32)
    homolog_rescaled = layer_normalize(homolog_matrix.astype(jnp.float32)).astype(jnp.bfloat16)
    homolog_lines_merged = homolog_rescaled.reshape(
        sequence_local_rows * residue_total, alignment_width
    )
    projected_rows = jnp.dot(
        homolog_lines_merged, tensor_factor_coefficients, preferred_element_type=jnp.float32
    ).reshape(sequence_local_rows, residue_total, 2 * opm_width)
    left_factor = (
        (projected_rows[..., :opm_width] * active_entry_mask[..., None])
        .astype(jnp.bfloat16)
        .reshape(sequence_local_rows, residue_total * opm_width)
    )
    right_factor = (
        (projected_rows[..., opm_width:] * active_entry_mask[..., None])
        .astype(jnp.bfloat16)
        .reshape(sequence_local_rows, residue_total * opm_width)
    )
    live_weights = active_entry_mask.astype(jnp.bfloat16)
    left_all, right_all, live_all = (
        lax.all_gather(left_factor, "row", axis=0, tiled=True),
        lax.all_gather(right_factor, "row", axis=0, tiled=True),
        lax.all_gather(live_weights, "row", axis=0, tiled=True),
    )
    left_cols = lax.dynamic_slice_in_dim(left_all, row_start * opm_width, res_local * opm_width, 1)
    live_cols = lax.dynamic_slice_in_dim(live_all, row_start, res_local, 1)
    outer_sum = lax.dot_general(left_cols, right_all, contract, preferred_element_type=jnp.float32)
    pair_count = lax.dot_general(live_cols, live_all, contract, preferred_element_type=jnp.float32)
    outer_flat = outer_sum.reshape(res_local, opm_width, residue_total, opm_width).transpose(
        0, 2, 1, 3
    )
    outer_flat = outer_flat.reshape(res_local * residue_total, opm_width * opm_width).astype(
        jnp.bfloat16
    )
    opm_update = jnp.dot(
        outer_flat, outer_output_weight, preferred_element_type=jnp.float32
    ).reshape(res_local, residue_total, pair_width)
    opm_update = opm_update / (0.001 + pair_count[..., None])
    chain_rows = lax.dynamic_slice_in_dim(chain_label, row_start, res_local, 0)
    index_rows = lax.dynamic_slice_in_dim(residue_number_index, row_start, res_local, 0)
    same_chain = chain_rows[:, None] == chain_label[None, :]
    offsets = (
        jnp.clip(index_rows[:, None] - residue_number_index[None, :], -REL_MAX, REL_MAX) + REL_MAX
    )
    bin_index = jnp.where(same_chain, offsets, 2 * REL_MAX + 1)
    one_hot = (
        (bin_index[..., None] == jnp.arange(table_rows, dtype=jnp.int32))
        .astype(jnp.float32)
        .reshape(-1, table_rows)
    )
    position_term = jnp.dot(
        one_hot, relative_position_table, precision=lax.Precision.HIGHEST
    ).reshape(res_local, residue_total, pair_width)
    updated = (pair_state_input.astype(jnp.float32) + position_term + opm_update).astype(
        jnp.bfloat16
    )
    pair_norm = layer_normalize(updated.astype(jnp.float32)).astype(jnp.bfloat16)
    pair_flat = pair_norm.reshape(res_local * residue_total, pair_width)
    head_bias = jnp.dot(pair_flat, pair_bias_weight, preferred_element_type=jnp.float32).astype(
        jnp.bfloat16
    )
    head_bias = head_bias.reshape(res_local, residue_total, head_total).transpose(2, 0, 1)
    full_bias = lax.all_gather(head_bias, "row", axis=1, tiled=True)
    tri_projected = jnp.dot(pair_flat, triangle_input_weight, preferred_element_type=jnp.float32)
    tri_left = (
        jax.nn.sigmoid(tri_projected[:, :tri_width]) * tri_projected[:, tri_width : 2 * tri_width]
    ).astype(jnp.bfloat16)
    tri_right = (
        jax.nn.sigmoid(tri_projected[:, 2 * tri_width : 3 * tri_width])
        * tri_projected[:, 3 * tri_width :]
    ).astype(jnp.bfloat16)
    tri_left = tri_left.reshape(res_local, residue_total, tri_width).transpose(2, 0, 1)
    tri_right = tri_right.reshape(res_local, residue_total, tri_width).transpose(2, 0, 1)
    left_channels, right_channels = (
        lax.all_to_all(tri_left, "row", split_axis=0, concat_axis=1, tiled=True),
        lax.all_to_all(tri_right, "row", split_axis=0, concat_axis=1, tiled=True),
    )
    channel_sum = jnp.einsum(
        "cki,ckj->cij", left_channels, right_channels, preferred_element_type=jnp.float32
    ).astype(jnp.bfloat16)
    row_sum = lax.all_to_all(channel_sum, "row", split_axis=1, concat_axis=0, tiled=True)
    tri_sum = row_sum.transpose(1, 2, 0)
    tri_normed = (
        layer_normalize(tri_sum.astype(jnp.float32))
        .astype(jnp.bfloat16)
        .reshape(res_local * residue_total, tri_width)
    )
    tri_gating = jax.nn.sigmoid(
        jnp.dot(pair_flat, triangle_output_gate, preferred_element_type=jnp.float32)
    )
    pair_state_output = updated.astype(jnp.float32).reshape(
        res_local * residue_total, pair_width
    ) + tri_gating * jnp.dot(tri_normed, triangle_output_weight, preferred_element_type=jnp.float32)
    pair_state_output = pair_state_output.astype(jnp.bfloat16).reshape(
        res_local, residue_total, pair_width
    )
    scorer_mapped_lines = jnp.dot(
        homolog_lines_merged, scorer_entry_coefficients, preferred_element_type=jnp.float32
    )
    asking_vectors = (
        scorer_mapped_lines[:, :alignment_width]
        .astype(jnp.bfloat16)
        .reshape(sequence_local_rows, residue_total, head_total, head_channel_width)
    )
    lookup_lines = (
        scorer_mapped_lines[:, alignment_width : 2 * alignment_width]
        .astype(jnp.bfloat16)
        .reshape(sequence_local_rows, residue_total, head_total, head_channel_width)
    )
    content_lines = (
        scorer_mapped_lines[:, 2 * alignment_width : 3 * alignment_width]
        .astype(jnp.bfloat16)
        .reshape(sequence_local_rows, residue_total, head_total, head_channel_width)
    )
    sigmoid_factor = (
        scorer_mapped_lines[:, 3 * alignment_width :]
        .astype(jnp.bfloat16)
        .reshape(sequence_local_rows, residue_total, head_total, head_channel_width)
    )
    mask_term = 1000000000.0 * (active_entry_mask - 1.0)
    score_scale = head_channel_width ** (-0.5)

    def attend(row_inputs):
        query_row, key_row, value_row, gate_row, mask_row = row_inputs
        scores = (
            jnp.einsum("ihd,jhd->hij", query_row, key_row, preferred_element_type=jnp.float32)
            * score_scale
        )
        scores = scores + full_bias.astype(jnp.float32) + mask_row[None, None, :]
        weights = jax.nn.softmax(scores, axis=-1).astype(jnp.bfloat16)
        attended = jnp.einsum(
            "hij,jhd->ihd", weights, value_row, preferred_element_type=jnp.float32
        )
        return (jax.nn.sigmoid(gate_row.astype(jnp.float32)) * attended).astype(jnp.bfloat16)

    sigmoid_scaled_lines = lax.map(
        attend, (asking_vectors, lookup_lines, content_lines, sigmoid_factor, mask_term)
    )
    homolog_revised = homolog_matrix.astype(jnp.float32).reshape(
        sequence_local_rows * residue_total, alignment_width
    ) + jnp.dot(
        sigmoid_scaled_lines.reshape(sequence_local_rows * residue_total, alignment_width),
        scorer_final_coefficients,
        preferred_element_type=jnp.float32,
    )
    homolog_revised = homolog_revised.astype(jnp.bfloat16).reshape(
        sequence_local_rows, residue_total, alignment_width
    )
    return (homolog_revised, pair_state_output)


def solution(mesh):
    return jax.shard_map(
        on_device,
        mesh=mesh,
        in_specs=(
            P(("grp", "row"), None, None),
            P(("grp", "row"), None),
            P(("grp", "row"), None, None),
            P("grp"),
            P("grp"),
            P(),
            P(),
            P(),
            P(),
            P(),
            P(),
            P(),
            P(),
            P(),
        ),
        out_specs=(P(("grp", "row"), None, None), P(("grp", "row"), None, None)),
        check_vma=False,
    )
```

profile of v0, /device:TPU:0, one launch (start us, length us, event | category | flops | bytes accessed | tf_op | source)
XLA Modules:
  0.0 210.1 jit_solution(4078920670390650498)
XLA Ops:
  0.6 1.1 convert_reduce_fusion
  1.7 1.1 multiply_reduce_fusion.2
  2.8 1.0 multiply_convert_fusion.2
  3.9 0.7 convert_bitcast_fusion
  4.6 0.9 fusion.51
  5.8 44.6 %all-gather = bf16[32,2,4096]{2,1,0:T(2,128)(2,1)S(1)} all-gather(bf16[1,2,4096]{2,1,0:T(2,128)(2,1)S(1)} %reshape.208), channel_id=1, replica_groups=mesh['grp'=1,'row'=32] {'row'}, dimensions={0}, use_global_device_ids=true | all-gather | bytes 540672 | tf_op jit(solution)/shard_map/all_gather | solution.py:64
  50.9 38.1 %all-gather.1 = bf16[32,2,4096]{2,1,0:T(2,128)(2,1)S(1)} all-gather(bf16[1,2,4096]{2,1,0:T(2,128)(2,1)S(1)} %reshape.210), channel_id=1, replica_groups=mesh['grp'=1,'row'=32] {'row'}, dimensions={0}, use_global_device_ids=true | all-gather | bytes 540672 | tf_op jit(solution)/shard_map/all_gather | solution.py:65
  89.2 0.5 convolution_convert_fusion
  89.7 4.5 %convert_element_type.106 = bf16[4,32,128,32]{3,2,1,0:T(8,128)(2,1)} reshape(bf16[128,4096]{1,0:T(8,128)(2,1)S(1)} %convolution_convert_fusion) | data formatting | bytes 2097152 | tf_op jit(solution)/shard_map/convert_element_type | solution.py:75
  94.1 3.6 %copy.75 = bf16[4,128,32,32]{1,3,2,0:T(8,128)(2,1)S(1)} copy(bf16[4,128,32,32]{3,1,2,0:T(8,128)(2,1)} %bitcast.135) | data formatting | bytes 2097152 | tf_op jit(solution)/shard_map/convert_element_type | solution.py:75
  97.7 37.9 %all-gather.2 = bf16[32,2,128]{2,1,0:T(2,128)(2,1)S(1)} all-gather(bf16[1,2,128]{2,1,0:T(2,128)(2,1)S(1)} %get-tuple-element.101), channel_id=1, replica_groups=mesh['grp'=1,'row'=32] {'row'}, dimensions={0}, use_global_device_ids=true | all-gather | bytes 16896 | tf_op jit(solution)/shard_map/all_gather | solution.py:66
  136.1 0.5 convolution_divide_fusion
  136.6 0.5 fusion.63
  137.6 0.3 fusion.64
  138.0 0.8 copy.83
  138.8 2.6 %all-to-all-start = ((bf16[128,4,128]{2,1,0:T(4,128)(2,1)}), bf16[128,4,128]{2,1,0:T(4,128)(2,1)S(1)}, u32[]{:S(2)}, u32[]{:S(2)}) async-start(bf16[128,4,128]{2,1,0:T(4,128)(2,1)} %bitcast.22), calls=%async_computation | async-start | bytes 262144 | tf_op jit(solution)/shard_map/all_to_all | solution.py:118
  141.5 0.3 convolution_convert_fusion.1
  141.9 42.5 %all_gather.15 = bf16[8,128,128]{2,0,1:T(8,128)(2,1)S(1)} all-gather(bf16[8,4,128]{2,0,1:T(8,128)(2,1)S(1)} %fusion.35), channel_id=1, replica_groups=mesh['grp'=1,'row'=32] {'row'}, dimensions={1}, use_global_device_ids=true | all-gather | bytes 270336 | tf_op jit(solution)/shard_map/all_gather | solution.py:106
  184.4 0.8 copy.86
  186.1 2.6 %all-to-all-start.1 = ((bf16[128,4,128]{2,1,0:T(4,128)(2,1)}), bf16[128,4,128]{2,1,0:T(4,128)(2,1)S(1)}, u32[]{:S(2)}, u32[]{:S(2)}) async-start(bf16[128,4,128]{2,1,0:T(4,128)(2,1)} %bitcast.27), calls=%async_computation.1 | async-start | bytes 262144 | tf_op jit(solution)/shard_map/all_to_all | solution.py:119
  188.8 2.0 while.10
  188.8 0.3 fusion.101
  189.1 0.4 fusion.100
  189.8 0.3 fusion.101
  190.1 0.4 fusion.100
  190.5 0.3 fusion.102
  190.9 6.1 %all-to-all-done.1 = bf16[128,4,128]{2,1,0:T(4,128)(2,1)S(1)} async-done(((bf16[128,4,128]{2,1,0:T(4,128)(2,1)}), bf16[128,4,128]{2,1,0:T(4,128)(2,1)S(1)}, u32[]{:S(2)}, u32[]{:S(2)}) %all-to-all-start.1) | async-done | bytes 131104 | tf_op jit(solution)/shard_map/all_to_all | solution.py:119
  197.3 0.8 copy.90
  198.1 2.6 %all-to-all-start.2 = ((bf16[4,128,128]{2,0,1:T(4,128)(2,1)}), bf16[4,128,128]{2,0,1:T(4,128)(2,1)S(1)}, u32[]{:S(2)}, u32[]{:S(2)}) async-start(bf16[4,128,128]{2,0,1:T(4,128)(2,1)} %copy.90), calls=%async_computation.2 | async-start | bytes 262144 | tf_op jit(solution)/shard_map/all_to_all | solution.py:124
  201.1 0.9 fusion.33
  202.0 6.9 %all-to-all-done.2 = bf16[4,128,128]{2,0,1:T(4,128)(2,1)S(1)} async-done(((bf16[4,128,128]{2,0,1:T(4,128)(2,1)}), bf16[4,128,128]{2,0,1:T(4,128)(2,1)S(1)}, u32[]{:S(2)}, u32[]{:S(2)}) %all-to-all-start.2) | async-done | bytes 131104 | tf_op jit(solution)/shard_map/all_to_all | solution.py:124
  209.2 0.8 fusion.34
  (79 shorter events, 4.5 us)
Async XLA Ops:
  0.6 140.9 %copy-start = (bf16[256,1024]{1,0:T(8,128)(2,1)S(1)}, bf16[256,1024]{1,0:T(8,128)(2,1)}, u32[]{:S(2)}) copy-start(bf16[256,1024]{1,0:T(8,128)(2,1)} %param.24) | copy-start | bytes 1572868
  89.6 46.2 %copy-start.10 = (s32[128]{0:T(128)S(1)}, s32[128]{0:T(128)}, u32[]{:S(2)}) copy-start(s32[128]{0:T(128)} %param.19) | copy-start | bytes 1540
  89.6 46.3 %copy-start.9 = (s32[128]{0:T(128)S(1)}, s32[128]{0:T(128)}, u32[]{:S(2)}) copy-start(s32[128]{0:T(128)} %param.20) | copy-start | bytes 1540
  89.6 46.4 %copy-start.11 = (bf16[1024,128]{1,0:T(8,128)(2,1)S(1)}, bf16[1024,128]{1,0:T(8,128)(2,1)}, u32[]{:S(2)}) copy-start(bf16[1024,128]{1,0:T(8,128)(2,1)} %param.23) | copy-start | bytes 786436
  94.1 42.5 %copy-start.3 = (bf16[4,128,128]{2,1,0:T(8,128)(2,1)S(1)}, bf16[4,128,128]{2,1,0:T(8,128)(2,1)}, u32[]{:S(2)}) copy-start(bf16[4,128,128]{2,1,0:T(8,128)(2,1)} %param.18) | copy-start | bytes 393220
  94.1 42.5 %copy-start.5 = (f32[66,128]{1,0:T(8,128)S(1)}, f32[66,128]{1,0:T(8,128)}, u32[]{:S(2)}) copy-start(f32[66,128]{1,0:T(8,128)} %param.21) | copy-start | bytes 101380
  94.1 43.4 %copy-start.2 = (bf16[128,512]{1,0:T(8,128)(2,1)S(1)}, bf16[128,512]{1,0:T(8,128)(2,1)}, u32[]{:S(2)}) copy-start(bf16[128,512]{1,0:T(8,128)(2,1)} %param.27) | copy-start | bytes 393220
  97.7 43.7 %copy-start.8 = (bf16[128,8]{0,1:T(8,128)(2,1)S(1)}, bf16[128,8]{0,1:T(8,128)(2,1)}, u32[]{:S(2)}) copy-start(bf16[128,8]{0,1:T(8,128)(2,1)} %param.26) | copy-start | bytes 6148
  137.8 48.3 %copy-start.7 = (s32[2,128]{1,0:T(2,128)S(1)}, s32[2,128]{1,0:T(2,128)}, u32[]{:S(2)}) copy-start(s32[2,128]{1,0:T(2,128)} %param.17) | copy-start | bytes 3076
  138.8 47.3 %all-to-all-start = ((bf16[128,4,128]{2,1,0:T(4,128)(2,1)}), bf16[128,4,128]{2,1,0:T(4,128)(2,1)S(1)}, u32[]{:S(2)}, u32[]{:S(2)}) async-start(bf16[128,4,128]{2,1,0:T(4,128)(2,1)} %bitcast.22), calls=%async_computation | async-start | bytes 262144 | tf_op jit(solution)/shard_map/all_to_all | solution.py:118
  186.1 10.8 %all-to-all-start.1 = ((bf16[128,4,128]{2,1,0:T(4,128)(2,1)}), bf16[128,4,128]{2,1,0:T(4,128)(2,1)S(1)}, u32[]{:S(2)}, u32[]{:S(2)}) async-start(bf16[128,4,128]{2,1,0:T(4,128)(2,1)} %bitcast.27), calls=%async_computation.1 | async-start | bytes 262144 | tf_op jit(solution)/shard_map/all_to_all | solution.py:119
  188.7 11.9 %copy-start.12 = (bf16[128,128]{1,0:T(8,128)(2,1)S(1)}, bf16[128,128]{1,0:T(8,128)(2,1)}, u32[]{:S(2)}) copy-start(bf16[128,128]{1,0:T(8,128)(2,1)} %param.28) | copy-start | bytes 98308
  188.8 12.3 %copy-start.1 = (bf16[2,128,256]{2,1,0:T(8,128)(2,1)S(1)}, bf16[2,128,256]{2,1,0:T(8,128)(2,1)}, u32[]{:S(2)}) copy-start(bf16[2,128,256]{2,1,0:T(8,128)(2,1)} %param.16) | copy-start | bytes 393220
  188.8 12.3 %copy-start.4 = (bf16[256,256]{1,0:T(8,128)(2,1)S(1)}, bf16[256,256]{1,0:T(8,128)(2,1)}, u32[]{:S(2)}) copy-start(bf16[256,256]{1,0:T(8,128)(2,1)} %param.25) | copy-start | bytes 393220
  190.8 18.5 %copy-start.6 = (bf16[128,128]{1,0:T(8,128)(2,1)S(1)}, bf16[128,128]{1,0:T(8,128)(2,1)}, u32[]{:S(2)}) copy-start(bf16[128,128]{1,0:T(8,128)(2,1)} %param.29) | copy-start | bytes 98308
  198.1 10.8 %all-to-all-start.2 = ((bf16[4,128,128]{2,0,1:T(4,128)(2,1)}), bf16[4,128,128]{2,0,1:T(4,128)(2,1)S(1)}, u32[]{:S(2)}, u32[]{:S(2)}) async-start(bf16[4,128,128]{2,0,1:T(4,128)(2,1)} %copy.90), calls=%async_computation.2 | async-start | bytes 262144 | tf_op jit(solution)/shard_map/all_to_all | solution.py:124
where the time goes:
time: 211 us; the launch traced here: 210 us
  blocking collectives  163 us (77%)
  local copies, waits for them, and re-layouts  13 us (6%)
  waiting for transfers between devices  13 us (6%)
  starting transfers between devices  7.74 us (4%)
  matrix products  7.36 us (3%)
  other arithmetic  4.76 us (2%)
    all_gather x1, blocking collectives, on_device(): lax.all_gather(left_factor, 'row', axis=0, tiled=True)  44.6 us
    all_gather x1, blocking collectives, on_device(): full_bias = lax.all_gather(head_bias, 'row', axis=1, tiled=True)  42.5 us
    all_gather x1, blocking collectives, on_device(): lax.all_gather(right_factor, 'row', axis=0, tiled=True)  38.1 us
    all_gather x1, blocking collectives, on_device(): lax.all_gather(live_weights, 'row', axis=0, tiled=True)  37.9 us
    convert_element_type x2, local copies, waits for them, and re-layouts, on_device(): outer_flat.reshape(res_local * residue_total, opm_width * opm_width)  8.06 us
    all_to_all x1, waiting for transfers between devices, on_device(): lax.all_to_all(channel_sum, 'row', split_axis=1, concat_axis=0, tiled=True)  6.94 us
    all_to_all x1, waiting for transfers between devices, on_device(): lax.all_to_all(tri_right, 'row', split_axis=0, concat_axis=1, tiled=True)  6.06 us
  transfers between devices with their start and end apart: 3, of which 2 were waited for; matrix products, arithmetic and copies ran while one was open for 3% of the time, Pallas kernels for 0%

commit v1 on v0

--- a/solution.py
+++ b/solution.py
@@ -1,9 +1,326 @@
+import functools
 import jax
 import jax.numpy as jnp
 from jax import lax
+from jax.experimental import pallas as pl
+from jax.experimental.pallas import tpu as pltpu
 from jax.sharding import PartitionSpec as P
 
 REL_MAX = 32
+F32 = jnp.float32
+BF16 = jnp.bfloat16
+OVER_FIRST = (((0,), (0,)), ((), ()))
+OVER_LAST = (((1,), (1,)), ((), ()))
+
+
+def mm(a, b):
+    return jnp.dot(a, b, preferred_element_type=F32)
+
+
+def norm_over(values, axis):
+    centre = jnp.mean(values, axis=axis, keepdims=True)
+    shifted = values - centre
+    spread = jnp.mean(shifted * shifted, axis=axis, keepdims=True)
+    return shifted * lax.rsqrt(spread + 1e-05)
+
+
+def fused(
+    n, msa, live_in, pair, chain, number, table, w_factor, w_outer, w_entry, w_final, w_bias, w_tri, w_gate, w_out,
+    msa_out, pair_out,
+    left_send, left_recv, right_send, right_recv, tri_send, tri_recv, bias_send, bias_recv, sum_send, sum_recv,
+    wide, outer_cat, w_outer_t, w_tri_t, base, qkvg, count, bias_wide,
+    send_sem, recv_sem,
+):
+    me = lax.axis_index("row")
+    rows, res, feats = msa.shape
+    own, _, cz = pair.shape
+    fac = w_factor.shape[1] // 2
+    heads = w_bias.shape[1]
+    span = feats // heads
+    tri = w_out.shape[0]
+    per = tri // n
+    chunk = right_send.shape[0]
+
+    barrier = pltpu.get_barrier_semaphore()
+
+    def greet(t, _):
+        pl.semaphore_signal(
+            barrier, inc=1, device_id={"row": lax.rem(me + t, n)}, device_id_type=pl.DeviceIdType.MESH
+        )
+        return 0
+
+    lax.fori_loop(1, n, greet, 0)
+
+    def copy_to(phase, t, src, dst):
+        return pltpu.make_async_remote_copy(
+            src_ref=src,
+            dst_ref=dst,
+            send_sem=send_sem.at[phase, t],
+            recv_sem=recv_sem.at[phase, me],
+            device_id={"row": lax.rem(me + t, n)},
+            device_id_type=pl.DeviceIdType.MESH,
+        )
+
+    def arrived(phase, t, src, dst):
+        return pltpu.make_async_remote_copy(
+            src_ref=src,
+            dst_ref=dst,
+            send_sem=send_sem.at[phase, t],
+            recv_sem=recv_sem.at[phase, lax.rem(me + t, n)],
+            device_id={"row": lax.rem(me + t, n)},
+            device_id_type=pl.DeviceIdType.MESH,
+        )
+
+    live = live_in[...].astype(F32)
+    factor_t = jnp.concatenate(
+        [jnp.transpose(w_factor[...].astype(F32)), jnp.zeros((2 * fac, feats), F32)], axis=0
+    ).astype(BF16)
+    normed = []
+    for s in range(rows):
+        normed.append(norm_over(msa[s].astype(F32), 1).astype(BF16))
+        factors = lax.dot_general(factor_t, normed[s], OVER_LAST, preferred_element_type=F32)
+        factors = factors * live[s : s + 1, :]
+        right_send[s * fac : (s + 1) * fac, :] = factors[fac : 2 * fac].astype(BF16)
+        wide[pl.ds(s, res, stride=rows), :] = jnp.transpose(factors)
+    right_send[rows * fac :, :] = jnp.concatenate(
+        [live, jnp.zeros((chunk - rows * fac - rows, res), F32)], axis=0
+    ).astype(BF16)
+    left_send[...] = wide[0 : res * rows, :].reshape(left_send.shape)
+
+    pl.semaphore_wait(barrier, n - 1)
+
+    def send_factors(t, _):
+        to = lax.rem(me + t, n)
+        copy_to(0, t, right_send, right_recv.at[me]).start()
+        copy_to(1, t, left_send.at[to], left_recv.at[me]).start()
+        return 0
+
+    lax.fori_loop(1, n, send_factors, 0)
+    right_recv[me] = right_send[...]
+    left_recv[me] = left_send[me]
+
+    wide[0 : fac * fac, :] = w_outer[...].astype(F32)
+    for e in range(fac):
+        outer_cat[e * fac : (e + 1) * fac, 0:cz] = wide[pl.ds(e, fac, stride=fac), :].astype(BF16)
+    w_outer_t[...] = jnp.transpose(outer_cat[:, 0:cz].astype(F32)).astype(BF16)
+    for b in range(4):
+        w_tri_t[b * tri : (b + 1) * tri, :] = jnp.transpose(
+            w_tri[:, b * tri : (b + 1) * tri].astype(F32)
+        ).astype(BF16)
+    gate_t = jnp.transpose(w_gate[...].astype(F32)).astype(BF16)
+    out_t = jnp.transpose(w_out[...].astype(F32)).astype(BF16)
+    for s in range(rows):
+        qkvg[s] = mm(normed[s], w_entry[...]).astype(BF16)
+    lane = lax.broadcasted_iota(jnp.int32, (1, res), 1)
+    bins = table.shape[0]
+    padded = table.shape[0] + (-table.shape[0]) % 8
+    slot = lax.broadcasted_iota(jnp.int32, (bins, res), 0).astype(F32)
+    chain_row = chain[...].astype(F32)
+    number_row = number[...].astype(F32)
+    for i in range(own):
+        mine = lane == me * own + i
+        chain_i = jnp.sum(jnp.where(mine, chain_row, 0.0), axis=1, keepdims=True)
+        number_i = jnp.sum(jnp.where(mine, number_row, 0.0), axis=1, keepdims=True)
+        offset = jnp.clip(number_i - number_row, -float(REL_MAX), float(REL_MAX)) + float(REL_MAX)
+        kind = jnp.where(chain_i == chain_row, offset, float(2 * REL_MAX + 1))
+        hot = jnp.where(slot == kind, 1.0, 0.0)
+        term = lax.dot_general(
+            table[...], hot, OVER_FIRST, precision=lax.Precision.HIGHEST, preferred_element_type=F32
+        )
+        base[:, i * res : (i + 1) * res] = jnp.transpose(pair[i].astype(F32)) + term
+
+    def wait_factors(t, _):
+        frm = lax.rem(me + t, n)
+        arrived(0, t, right_send, right_recv.at[frm]).wait()
+        arrived(1, t, left_send.at[frm], left_recv.at[frm]).wait()
+        return 0
+
+    lax.fori_loop(1, n, wait_factors, 0)
+
+    left_flat = left_recv.reshape(n * own * rows, cz)
+    left_rows = []
+    for i in range(own):
+        part = jnp.concatenate(
+            [left_flat[pl.ds(i * rows + s, n, stride=own * rows), :] for s in range(rows)], axis=0
+        )
+        left_rows.append(jnp.transpose(part)[0:fac])
+    left_t = jnp.concatenate(left_rows, axis=0).astype(BF16)
+    wide[0 : n * chunk, :] = right_recv[...].astype(F32).reshape(n * chunk, res)
+
+    def right_at(k):
+        return jnp.concatenate(
+            [wide[pl.ds(s * fac + k, n, stride=chunk), :] for s in range(rows)], axis=0
+        ).astype(BF16)
+
+    live_all = jnp.concatenate(
+        [wide[pl.ds(rows * fac + s, n, stride=chunk), :] for s in range(rows)], axis=0
+    )
+    count[...] = mm(jnp.transpose(live_all).astype(BF16), live_all.astype(BF16))
+    for e in range(fac):
+        product = mm(left_t, right_at(e)).astype(BF16)
+        for i in range(own):
+            outer_cat[e * fac : (e + 1) * fac, i * res : (i + 1) * res] = product[i * fac : (i + 1) * fac]
+    opm = mm(w_outer_t[...], outer_cat[...])
+    for i in range(own):
+        cols = slice(i * res, (i + 1) * res)
+        base[:, cols] = base[:, cols] + opm[:, cols] / (0.001 + count[pl.ds(me * own + i, 1), :])
+    updated = base[...].astype(BF16).astype(F32)
+    base[...] = updated
+    pair_norm = norm_over(updated, 0).astype(BF16)
+
+    projected = mm(w_tri_t[...], pair_norm)
+    both = (
+        jax.nn.sigmoid(projected[0:tri]) * projected[tri : 2 * tri],
+        jax.nn.sigmoid(projected[2 * tri : 3 * tri]) * projected[3 * tri :],
+    )
+    lines = 2 * per * own
+    for side in range(2):
+        for c in range(per):
+            for k in range(own):
+                wide[pl.ds((side * per + c) * own + k, n, stride=lines), :] = both[side][
+                    c * n : (c + 1) * n, k * res : (k + 1) * res
+                ]
+    tri_send[...] = wide[0 : n * lines, :].astype(BF16).reshape(tri_send.shape)
+    bias_t = lax.dot_general(w_bias[...], pair_norm, OVER_FIRST, preferred_element_type=F32)
+    bias_send[...] = jnp.concatenate(
+        [bias_t[:, i * res : (i + 1) * res] for i in range(own)], axis=0
+    ).astype(BF16)
+
+    def send_tri(t, _):
+        to = lax.rem(me + t, n)
+        copy_to(2, t, tri_send.at[to], tri_recv.at[me]).start()
+        return 0
+
+    def send_bias(t, _):
+        copy_to(3, t, bias_send, bias_recv.at[me]).start()
+        return 0
+
+    lax.fori_loop(1, n, send_tri, 0)
+    lax.fori_loop(1, n, send_bias, 0)
+    tri_recv[me] = tri_send[me]
+    bias_recv[me] = bias_send[...]
+    gating = jax.nn.sigmoid(mm(gate_t, pair_norm))
+
+    def wait_tri(t, _):
+        frm = lax.rem(me + t, n)
+        arrived(2, t, tri_send.at[frm], tri_recv.at[frm]).wait()
+        return 0
+
+    lax.fori_loop(1, n, wait_tri, 0)
+    wide[0 : n * lines, :] = tri_recv[...].astype(F32).reshape(n * lines, res)
+    sums = []
+    for c in range(per):
+        left_c, right_c = (
+            jnp.concatenate(
+                [wide[pl.ds((side * per + c) * own + k, n, stride=lines), :] for k in range(own)], axis=0
+            )
+            for side in range(2)
+        )
+        sums.append(mm(jnp.transpose(left_c).astype(BF16), right_c.astype(BF16)))
+    for c in range(per):
+        wide[pl.ds(c, res, stride=per), :] = sums[c]
+    sum_send[...] = wide[0 : res * per, :].astype(BF16).reshape(sum_send.shape)
+
+    def send_sum(t, _):
+        to = lax.rem(me + t, n)
+        copy_to(4, t, sum_send.at[to], sum_recv.at[me]).start()
+        return 0
+
+    lax.fori_loop(1, n, send_sum, 0)
+    sum_recv[me] = sum_send[me]
+
+    def wait_bias(t, _):
+        frm = lax.rem(me + t, n)
+        arrived(3, t, bias_send, bias_recv.at[frm]).wait()
+        return 0
+
+    lax.fori_loop(1, n, wait_bias, 0)
+    bias_wide[...] = bias_recv[...].astype(F32).reshape(bias_wide.shape)
+    column = lax.broadcasted_iota(jnp.int32, (1, feats), 1)
+    scale = span ** (-0.5)
+    for s in range(rows):
+        query = qkvg[s, :, 0:feats]
+        key = qkvg[s, :, feats : 2 * feats]
+        value = qkvg[s, :, 2 * feats : 3 * feats]
+        gate = jax.nn.sigmoid(qkvg[s, :, 3 * feats :].astype(F32))
+        mask = 1000000000.0 * (live[s : s + 1, :] - 1.0)
+        attended = jnp.zeros((res, feats), F32)
+        for h in range(heads):
+            at_head = (column >= h * span) & (column < (h + 1) * span)
+            scores = lax.dot_general(
+                jnp.where(at_head, query, jnp.zeros_like(query)), key, OVER_LAST, preferred_element_type=F32
+            )
+            scores = scores * scale + bias_wide[pl.ds(h, res, stride=heads), :] + mask
+            scores = jnp.exp(scores - jnp.max(scores, axis=1, keepdims=True))
+            weights = (scores / jnp.sum(scores, axis=1, keepdims=True)).astype(BF16)
+            attended = jnp.where(at_head, mm(weights, value), attended)
+        gated = (gate * attended).astype(BF16)
+        msa_out[s] = (msa[s].astype(F32) + mm(gated, w_final[...])).astype(BF16)
+
+    def wait_sum(t, _):
+        frm = lax.rem(me + t, n)
+        arrived(4, t, sum_send.at[frm], sum_recv.at[frm]).wait()
+        return 0
+
+    lax.fori_loop(1, n, wait_sum, 0)
+    wide[0 : res * per, :] = sum_recv[...].astype(F32).reshape(res * per, res)
+    for i in range(own):
+        tri_sum = jnp.concatenate(
+            [wide[pl.ds(i * per + c, n, stride=own * per), :] for c in range(per)], axis=0
+        )
+        tri_normed = norm_over(tri_sum, 0).astype(BF16)
+        cols = slice(i * res, (i + 1) * res)
+        result = base[:, cols] + gating[:, cols] * mm(out_t, tri_normed)
+        pair_out[i] = jnp.transpose(result).astype(BF16)
+
+
+def fused_on_device(
+    n, msa, live, pair, chain, number, table, w_factor, w_outer, w_entry, w_final, w_bias, w_tri, w_gate, w_out
+):
+    rows, res, feats = msa.shape
+    own, _, cz = pair.shape
+    fac = w_factor.shape[1] // 2
+    heads = w_bias.shape[1]
+    tri = w_out.shape[0]
+    per = tri // n
+    chunk = rows * fac + 16
+    lines = 2 * per * own
+    wide_rows = max(n * chunk, n * lines, fac * fac, rows * res, per * res)
+    vmem = pl.BlockSpec(memory_space=pltpu.VMEM)
+    return pl.pallas_call(
+        functools.partial(fused, n),
+        out_shape=(jax.ShapeDtypeStruct(msa.shape, BF16), jax.ShapeDtypeStruct(pair.shape, BF16)),
+        in_specs=[vmem] * 14,
+        out_specs=(vmem, vmem),
+        scratch_shapes=[
+            pltpu.VMEM((n, own * rows, res), F32),
+            pltpu.VMEM((n, own * rows, res), F32),
+            pltpu.VMEM((chunk, res), BF16),
+            pltpu.VMEM((n, chunk, res), BF16),
+            pltpu.VMEM((n, lines, res), BF16),
+            pltpu.VMEM((n, lines, res), BF16),
+            pltpu.VMEM((own * heads, res), BF16),
+            pltpu.VMEM((n, own * heads, res), BF16),
+            pltpu.VMEM((n, own * per, res), BF16),
+            pltpu.VMEM((n, own * per, res), BF16),
+            pltpu.VMEM((wide_rows, res), F32),
+            pltpu.VMEM((fac * fac, own * res), BF16),
+            pltpu.VMEM((cz, fac * fac), BF16),
+            pltpu.VMEM((4 * tri, cz), BF16),
+            pltpu.VMEM((cz, own * res), F32),
+            pltpu.VMEM((rows, res, 4 * feats), BF16),
+            pltpu.VMEM((res, res), F32),
+            pltpu.VMEM((n * own * heads, res), F32),
+            pltpu.SemaphoreType.DMA((5, n)),
+            pltpu.SemaphoreType.DMA((5, n)),
+        ],
+        compiler_params=pltpu.CompilerParams(
+            collective_id=0, has_side_effects=True, vmem_limit_bytes=48 * 1024 * 1024
+        ),
+    )(
+        msa, live, pair, chain.reshape(1, res), number.reshape(1, res), table,
+        w_factor, w_outer, w_entry, w_final, w_bias, w_tri, w_gate, w_out,
+    )
 
 
 def layer_normalize(values):
@@ -193,8 +510,21 @@
 
 
 def solution(mesh):
+    n = mesh.shape["row"]
+
+    def body(*blocks):
+        msa, pair, w_out = blocks[0], blocks[2], blocks[13]
+        rows, res, _ = msa.shape
+        fits = (
+            res == pair.shape[2] == w_out.shape[0] == 128
+            and res % n == 0
+            and w_out.shape[0] % n == 0
+            and (res // n) * rows == 8
+        )
+        return fused_on_device(n, *blocks) if fits else on_device(*blocks)
+
     return jax.shard_map(
-        on_device,
+        body,
         mesh=mesh,
         in_specs=(
             P(("grp", "row"), None, None),

time: 211 us -> 57.4 us (0.27)
  blocking collectives: 163 us -> 0 us
  Pallas kernels: 0 us -> 46.1 us
  waiting for transfers between devices: 13 us -> 0 us
  starting transfers between devices: 7.74 us -> 0 us
  matrix products: 7.36 us -> 0 us
  other arithmetic: 4.76 us -> 0 us
  local copies, waits for them, and re-layouts: 13 us -> 9.99 us
    all_gather x4 -> x0, blocking collectives: 163 us -> none  [the longest x1 44.6 us: on_device(): lax.all_gather(left_factor, 'row', axis=0, tiled=True)]
    pallas_call x0 -> x1, Pallas kernels: none -> 46.1 us  [fused_on_device(): pl.pallas_call(functools.partial(fused, n), out_shape=(jax.ShapeDtypeStru...]
    all_to_all x3 -> x0, waiting for transfers between devices: 13 us -> none  [the longest x1 6.94 us: on_device(): lax.all_to_all(channel_sum, 'row', split_axis=1, concat_axis=0, tiled=True)]
    unnamed x30, local copies, waits for them, and re-layouts: 0.72 us -> 9.99 us
    convert_element_type x7 -> x0, local copies, waits for them, and re-layouts: 9.23 us -> none  [the longest x2 8.06 us: on_device(): outer_flat.reshape(res_local * residue_total, opm_width * opm_width)]
    all_to_all x3 -> x0, starting transfers between devices: 7.74 us -> none  [the longest x1 2.59 us: on_device(): lax.all_to_all(tri_right, 'row', split_axis=0, concat_axis=1, tiled=True)]
    dot_general x16 -> x0, matrix products: 6.56 us -> none  [the longest x1 0.91 us: on_device(): jnp.dot(homolog_lines_merged, tensor_factor_coefficients, preferred_eleme...]
    reduce_sum x5 -> x0, other arithmetic: 2.48 us -> none  [the longest x3 1.37 us: layer_normalize(): spread = jnp.mean(shifted * shifted, axis=-1, keepdims=True)]
  transfers between devices with their start and end apart: 3 -> 0, of which waited for: 2 -> 0; matrix products, arithmetic and copies ran while one was open for 3% -> 0% of each run, Pallas kernels for 0% -> 0%
where the time goes in v1:
time: 57.4 us; the launch traced here: 56.8 us
  Pallas kernels  46.1 us (80%)
  local copies, waits for them, and re-layouts  9.99 us (17%)
  between operations  0.72 us (1%)
    pallas_call x1, Pallas kernels, fused_on_device(): pl.pallas_call(functools.partial(fused, n), out_shape=(jax.ShapeDtypeStru...  46.1 us
    unnamed x30, local copies, waits for them, and re-layouts  9.99 us

profile of v1, /device:TPU:0, one launch (start us, length us, event | category | flops | bytes accessed | tf_op | source)
XLA Modules:
  0.0 56.8 jit_solution(13946847133270435220)
XLA Ops:
  0.6 0.0 copy-start.12
  0.6 0.0 copy-start.2
  0.6 0.7 %copy-done.12 = bf16[128,8]{0,1:T(8,128)(2,1)S(1)} copy-done((bf16[128,8]{0,1:T(8,128)(2,1)S(1)}, bf16[128,8]{0,1:T(8,128)(2,1)}, u32[]{:S(2)}) %copy-start.12) | copy-done | bytes 2072
  1.3 0.1 copy.17.w_bias
  1.4 0.0 copy-start.9
  1.4 0.0 copy-start.10
  1.5 0.0 copy-start.11
  1.5 0.9 %copy.16.w_factor = bf16[256,64]{1,0:T(8,128)(2,1)S(1)} copy(bf16[256,64]{0,1:T(8,128)(2,1)} %param.20) | data formatting | bytes 65536 | tf_op args[6]
  2.4 0.0 copy-done.2
  2.4 0.0 copy-done.9
  2.4 0.0 copy-done.10
  2.4 0.0 copy-done.11
  2.4 0.0 copy-start
  2.4 1.0 %copy-done = bf16[256,1024]{1,0:T(8,128)(2,1)S(1)} copy-done((bf16[256,1024]{1,0:T(8,128)(2,1)S(1)}, bf16[256,1024]{1,0:T(8,128)(2,1)}, u32[]{:S(2)}) %copy-start) | copy-done | bytes 524312
  3.4 0.0 copy-start.1
  3.4 0.9 %copy-done.1 = bf16[1024,128]{1,0:T(8,128)(2,1)S(1)} copy-done((bf16[1024,128]{1,0:T(8,128)(2,1)S(1)}, bf16[1024,128]{1,0:T(8,128)(2,1)}, u32[]{:S(2)}) %copy-start.1) | copy-done | bytes 262168
  4.4 0.0 copy-start.3
  4.4 0.9 %copy-done.3 = bf16[4,128,128]{2,1,0:T(8,128)(2,1)S(1)} copy-done((bf16[4,128,128]{2,1,0:T(8,128)(2,1)S(1)}, bf16[4,128,128]{2,1,0:T(8,128)(2,1)}, u32[]{:S(2)}) %copy-start.3) | copy-done | bytes 131096
  5.3 0.0 copy-start.4
  5.3 0.9 %copy-done.4 = bf16[256,256]{1,0:T(8,128)(2,1)S(1)} copy-done((bf16[256,256]{1,0:T(8,128)(2,1)S(1)}, bf16[256,256]{1,0:T(8,128)(2,1)}, u32[]{:S(2)}) %copy-start.4) | copy-done | bytes 131096
  6.2 0.0 copy-start.5
  6.2 0.9 %copy-done.5 = bf16[128,512]{1,0:T(8,128)(2,1)S(1)} copy-done((bf16[128,512]{1,0:T(8,128)(2,1)S(1)}, bf16[128,512]{1,0:T(8,128)(2,1)}, u32[]{:S(2)}) %copy-start.5) | copy-done | bytes 131096
  7.1 0.0 copy-start.6
  7.1 0.8 %copy-done.6 = f32[66,128]{1,0:T(8,128)S(1)} copy-done((f32[66,128]{1,0:T(8,128)S(1)}, f32[66,128]{1,0:T(8,128)}, u32[]{:S(2)}) %copy-start.6) | copy-done | bytes 33816
  7.9 0.0 copy-start.7
  7.9 0.8 %copy-done.7 = bf16[128,128]{1,0:T(8,128)(2,1)S(1)} copy-done((bf16[128,128]{1,0:T(8,128)(2,1)S(1)}, bf16[128,128]{1,0:T(8,128)(2,1)}, u32[]{:S(2)}) %copy-start.7) | copy-done | bytes 32792
  8.6 0.0 copy-start.8
  8.6 0.8 %copy-done.8 = bf16[128,128]{1,0:T(8,128)(2,1)S(1)} copy-done((bf16[128,128]{1,0:T(8,128)(2,1)S(1)}, bf16[128,128]{1,0:T(8,128)(2,1)}, u32[]{:S(2)}) %copy-start.8) | copy-done | bytes 32792
  9.4 46.1 %shard_map.149 = (bf16[2,128,256]{2,1,0:T(8,128)(2,1)S(1)}, bf16[4,128,128]{2,1,0:T(8,128)(2,1)S(1)}) custom-call(bf16[2,128,256]{2,1,0:T(8,128)(2,1)S(1)} %copy-done.2, s32[2,128]{1,0:T(2,128)S(1)} %copy-done.9, bf16[4,128,128]{2,1,0:T(8,128)(2,1)S(1)} %copy-done.3, s32[1,128]{1,0:T(1,128)S(1)} %bitcast.2, s32[1,128]{1,0:T(1,128)S(1)} %bitcast.3, ...), custom_call_target="tpu_custom_call" | custom-call | tf_op jit(solution)/shard_map/pallas_call | solution.py:290
  55.5 0.7 %copy.20 = bf16[2,128,256]{2,1,0:T(8,128)(2,1)} copy(bf16[2,128,256]{2,1,0:T(8,128)(2,1)S(1)} %get-tuple-element.4) | data formatting | bytes 262144
  56.2 0.7 %copy.21 = bf16[4,128,128]{2,1,0:T(8,128)(2,1)} copy(bf16[4,128,128]{2,1,0:T(8,128)(2,1)S(1)} %get-tuple-element.5) | data formatting | bytes 262144
Async XLA Ops:
  0.6 0.7 %copy-start.12 = (bf16[128,8]{0,1:T(8,128)(2,1)S(1)}, bf16[128,8]{0,1:T(8,128)(2,1)}, u32[]{:S(2)}) copy-start(bf16[128,8]{0,1:T(8,128)(2,1)} %param.24) | copy-start | bytes 6148
  0.6 1.7 %copy-start.2 = (bf16[2,128,256]{2,1,0:T(8,128)(2,1)S(1)}, bf16[2,128,256]{2,1,0:T(8,128)(2,1)}, u32[]{:S(2)}) copy-start(bf16[2,128,256]{2,1,0:T(8,128)(2,1)} %msa.1) | copy-start | bytes 393220
  1.4 0.9 %copy-start.9 = (s32[2,128]{1,0:T(2,128)S(1)}, s32[2,128]{1,0:T(2,128)}, u32[]{:S(2)}) copy-start(s32[2,128]{1,0:T(2,128)} %live_in.1) | copy-start | bytes 3076
  1.4 0.9 %copy-start.10 = (s32[128]{0:T(128)S(1)}, s32[128]{0:T(128)}, u32[]{:S(2)}) copy-start(s32[128]{0:T(128)} %param.17) | copy-start | bytes 1540
  1.5 0.9 %copy-start.11 = (s32[128]{0:T(128)S(1)}, s32[128]{0:T(128)}, u32[]{:S(2)}) copy-start(s32[128]{0:T(128)} %param.18) | copy-start | bytes 1540
  2.4 1.0 %copy-start = (bf16[256,1024]{1,0:T(8,128)(2,1)S(1)}, bf16[256,1024]{1,0:T(8,128)(2,1)}, u32[]{:S(2)}) copy-start(bf16[256,1024]{1,0:T(8,128)(2,1)} %w_entry.1) | copy-start | bytes 1572868
  3.4 0.9 %copy-start.1 = (bf16[1024,128]{1,0:T(8,128)(2,1)S(1)}, bf16[1024,128]{1,0:T(8,128)(2,1)}, u32[]{:S(2)}) copy-start(bf16[1024,128]{1,0:T(8,128)(2,1)} %w_outer.1) | copy-start | bytes 786436
  4.4 0.9 %copy-start.3 = (bf16[4,128,128]{2,1,0:T(8,128)(2,1)S(1)}, bf16[4,128,128]{2,1,0:T(8,128)(2,1)}, u32[]{:S(2)}) copy-start(bf16[4,128,128]{2,1,0:T(8,128)(2,1)} %pair.1) | copy-start | bytes 393220
  5.3 0.9 %copy-start.4 = (bf16[256,256]{1,0:T(8,128)(2,1)S(1)}, bf16[256,256]{1,0:T(8,128)(2,1)}, u32[]{:S(2)}) copy-start(bf16[256,256]{1,0:T(8,128)(2,1)} %w_final.1) | copy-start | bytes 393220
  6.2 0.9 %copy-start.5 = (bf16[128,512]{1,0:T(8,128)(2,1)S(1)}, bf16[128,512]{1,0:T(8,128)(2,1)}, u32[]{:S(2)}) copy-start(bf16[128,512]{1,0:T(8,128)(2,1)} %w_tri.1) | copy-start | bytes 393220
  7.1 0.8 %copy-start.6 = (f32[66,128]{1,0:T(8,128)S(1)}, f32[66,128]{1,0:T(8,128)}, u32[]{:S(2)}) copy-start(f32[66,128]{1,0:T(8,128)} %table.1) | copy-start | bytes 101380
  7.9 0.8 %copy-start.7 = (bf16[128,128]{1,0:T(8,128)(2,1)S(1)}, bf16[128,128]{1,0:T(8,128)(2,1)}, u32[]{:S(2)}) copy-start(bf16[128,128]{1,0:T(8,128)(2,1)} %w_gate.1) | copy-start | bytes 98308
  8.6 0.8 %copy-start.8 = (bf16[128,128]{1,0:T(8,128)(2,1)S(1)}, bf16[128,128]{1,0:T(8,128)(2,1)}, u32[]{:S(2)}) copy-start(bf16[128,128]{1,0:T(8,128)(2,1)} %w_out.1) | copy-start | bytes 98308

commit v2 on v1

--- a/solution.py
+++ b/solution.py
@@ -9,6 +9,7 @@
 REL_MAX = 32
 F32 = jnp.float32
 BF16 = jnp.bfloat16
+LEFT = jnp.bfloat16
 OVER_FIRST = (((0,), (0,)), ((), ()))
 OVER_LAST = (((1,), (1,)), ((), ()))
 
@@ -25,17 +26,31 @@
 
 
 def fused(
-    n, msa, live_in, pair, chain, number, table, w_factor, w_outer, w_entry, w_final, w_bias, w_tri, w_gate, w_out,
-    msa_out, pair_out,
+    n, *refs
+):
+    inputs, (msa_out, pair_out), landed = refs[:14], refs[14:16], refs[16:30]
+    fused_body(n, inputs, landed, msa_out, pair_out, *refs[30:])
+
+
+def fused_body(
+    n, inputs, landed, msa_out, pair_out,
     left_send, left_recv, right_send, right_recv, tri_send, tri_recv, bias_send, bias_recv, sum_send, sum_recv,
-    wide, outer_cat, w_outer_t, w_tri_t, base, qkvg, count, bias_wide,
-    send_sem, recv_sem,
+    wide, outer_cat, w_outer_t, w_tri_t, base, qkvg, count, bias_wide, outer_wide,
+    send_sem, recv_sem, load_sem,
 ):
+    msa, live_in, pair, chain, number, table, w_factor, w_outer, w_entry, w_final, w_bias, w_tri, w_gate, w_out = landed
     me = lax.axis_index("row")
+    core = lax.rem(me, 2)
+    chip = me // 2
+    chips = n // 2
+    sibling = me + 1 - 2 * core
+    loads = [pltpu.make_async_copy(inputs[k], landed[k], load_sem.at[k]) for k in range(14)]
+    for k in (0, 1, 6, 7, 8, 2, 11, 3, 4, 5, 12, 13, 9, 10):
+        loads[k].start()
     rows, res, feats = msa.shape
     own, _, cz = pair.shape
-    fac = w_factor.shape[1] // 2
-    heads = w_bias.shape[1]
+    fac = w_factor.shape[0] // 2
+    heads = w_bias.shape[0]
     span = feats // heads
     tri = w_out.shape[0]
     per = tri // n
@@ -71,38 +86,86 @@
             device_id_type=pl.DeviceIdType.MESH,
         )
 
+    for k in (0, 1, 6):
+        loads[k].wait()
     live = live_in[...].astype(F32)
     factor_t = jnp.concatenate(
-        [jnp.transpose(w_factor[...].astype(F32)), jnp.zeros((2 * fac, feats), F32)], axis=0
+        [w_factor[...].astype(F32), jnp.zeros((2 * fac, feats), F32)], axis=0
     ).astype(BF16)
     normed = []
+    base_row = n * chunk
+    wide[base_row : base_row + 8 * n, :] = jnp.zeros((8 * n, res), F32)
     for s in range(rows):
         normed.append(norm_over(msa[s].astype(F32), 1).astype(BF16))
         factors = lax.dot_general(factor_t, normed[s], OVER_LAST, preferred_element_type=F32)
         factors = factors * live[s : s + 1, :]
         right_send[s * fac : (s + 1) * fac, :] = factors[fac : 2 * fac].astype(BF16)
-        wide[pl.ds(s, res, stride=rows), :] = jnp.transpose(factors)
-    right_send[rows * fac :, :] = jnp.concatenate(
-        [live, jnp.zeros((chunk - rows * fac - rows, res), F32)], axis=0
-    ).astype(BF16)
-    left_send[...] = wide[0 : res * rows, :].reshape(left_send.shape)
+        count[...] = jnp.transpose(
+            jnp.concatenate([factors[0:fac], jnp.zeros((res - fac, res), F32)], axis=0)
+        )
+        packed = count[pl.ds(0, n, stride=own), :]
+        for i in range(1, own):
+            packed = packed + pltpu.roll(count[pl.ds(i, n, stride=own), :], i * fac, 1)
+        wide[pl.ds(base_row + s, n, stride=8), :] = packed
+        wide[pl.ds(base_row + rows + s, n, stride=8), :] = jnp.broadcast_to(live[s : s + 1, :], (n, res))
+    left_send[...] = wide[base_row : base_row + 8 * n, :].astype(left_send.dtype).reshape(left_send.shape)
 
     pl.semaphore_wait(barrier, n - 1)
 
-    def send_factors(t, _):
+    def to_device(src, dst, out_sem, in_sem, device):
+        return pltpu.make_async_remote_copy(
+            src_ref=src, dst_ref=dst, send_sem=out_sem, recv_sem=in_sem,
+            device_id={"row": device}, device_id_type=pl.DeviceIdType.MESH,
+        )
+
+    def right_out(t):
+        to = lax.rem(chip + t, chips) * 2 + core
+        return to_device(right_send, right_recv.at[me], send_sem.at[0, t], recv_sem.at[0, me], to)
+
+    def right_on(t):
+        frm = lax.rem(chip + chips - t, chips) * 2 + core
+        return to_device(
+            right_recv.at[frm], right_recv.at[frm], send_sem.at[0, chips + t], recv_sem.at[0, frm], sibling
+        )
+
+    def right_in(frm):
+        return to_device(right_send, right_recv.at[frm], send_sem.at[0, 0], recv_sem.at[0, frm], sibling)
+
+    def send_right(t, _):
+        right_out(t).start()
+        return 0
+
+    def send_left(t, _):
         to = lax.rem(me + t, n)
-        copy_to(0, t, right_send, right_recv.at[me]).start()
         copy_to(1, t, left_send.at[to], left_recv.at[me]).start()
         return 0
 
-    lax.fori_loop(1, n, send_factors, 0)
+    def widen_right(frm):
+        wide[pl.ds(pl.multiple_of(frm * chunk, chunk), chunk), :] = right_recv[frm].astype(F32)
+
+    def hand_on(t, _):
+        frm = lax.rem(chip + chips - t, chips) * 2 + core
+        right_in(frm).wait_recv()
+        right_on(t).start()
+        widen_right(frm)
+        return 0
+
+    lax.fori_loop(1, chips, send_right, 0)
+    to_sibling = to_device(right_send, right_recv.at[me], send_sem.at[0, 0], recv_sem.at[0, me], sibling)
+    to_sibling.start()
+    lax.fori_loop(1, n, send_left, 0)
     right_recv[me] = right_send[...]
+    widen_right(me)
     left_recv[me] = left_send[me]
 
-    wide[0 : fac * fac, :] = w_outer[...].astype(F32)
+    loads[7].wait()
+    outer_wide[...] = w_outer[...].astype(F32)
     for e in range(fac):
-        outer_cat[e * fac : (e + 1) * fac, 0:cz] = wide[pl.ds(e, fac, stride=fac), :].astype(BF16)
+        outer_cat[e * fac : (e + 1) * fac, 0:cz] = outer_wide[pl.ds(e, fac, stride=fac), :].astype(BF16)
     w_outer_t[...] = jnp.transpose(outer_cat[:, 0:cz].astype(F32)).astype(BF16)
+    lax.fori_loop(1, 1 + chips // 4, hand_on, 0)
+    for k in (8, 11, 12, 13):
+        loads[k].wait()
     for b in range(4):
         w_tri_t[b * tri : (b + 1) * tri, :] = jnp.transpose(
             w_tri[:, b * tri : (b + 1) * tri].astype(F32)
@@ -111,6 +174,9 @@
     out_t = jnp.transpose(w_out[...].astype(F32)).astype(BF16)
     for s in range(rows):
         qkvg[s] = mm(normed[s], w_entry[...]).astype(BF16)
+    lax.fori_loop(1 + chips // 4, 1 + chips // 2, hand_on, 0)
+    for k in (2, 3, 4, 5):
+        loads[k].wait()
     lane = lax.broadcasted_iota(jnp.int32, (1, res), 1)
     bins = table.shape[0]
     padded = table.shape[0] + (-table.shape[0]) % 8
@@ -129,41 +195,46 @@
         )
         base[:, i * res : (i + 1) * res] = jnp.transpose(pair[i].astype(F32)) + term
 
-    def wait_factors(t, _):
+    lax.fori_loop(1 + chips // 2, chips, hand_on, 0)
+
+    def wait_left(t, _):
         frm = lax.rem(me + t, n)
-        arrived(0, t, right_send, right_recv.at[frm]).wait()
-        arrived(1, t, left_send.at[frm], left_recv.at[frm]).wait()
-        return 0
-
-    lax.fori_loop(1, n, wait_factors, 0)
-
-    left_flat = left_recv.reshape(n * own * rows, cz)
-    left_rows = []
-    for i in range(own):
-        part = jnp.concatenate(
-            [left_flat[pl.ds(i * rows + s, n, stride=own * rows), :] for s in range(rows)], axis=0
-        )
-        left_rows.append(jnp.transpose(part)[0:fac])
-    left_t = jnp.concatenate(left_rows, axis=0).astype(BF16)
-    wide[0 : n * chunk, :] = right_recv[...].astype(F32).reshape(n * chunk, res)
+        arrived(1, t, left_send.at[frm], left_recv.at[frm]).wait_recv()
+        return 0
+
+    def wait_sibling(t, _):
+        frm = lax.rem(chip + chips - t, chips) * 2 + 1 - core
+        right_in(frm).wait_recv()
+        widen_right(frm)
+        return 0
+
+    lax.fori_loop(1, n, wait_left, 0)
+
+    wide[base_row : base_row + 8 * n, :] = left_recv[...].astype(F32).reshape(8 * n, res)
+    left_rows, live_rows = (
+        jnp.concatenate([wide[pl.ds(base_row + r + s, n, stride=8), :] for s in range(rows)], axis=0)
+        for r in (0, rows)
+    )
+    left_t = jnp.transpose(left_rows).astype(BF16)
+    count[...] = mm(jnp.transpose(live_rows).astype(BF16), live_rows.astype(BF16))
+    lax.fori_loop(0, chips, wait_sibling, 0)
 
     def right_at(k):
         return jnp.concatenate(
             [wide[pl.ds(s * fac + k, n, stride=chunk), :] for s in range(rows)], axis=0
         ).astype(BF16)
 
-    live_all = jnp.concatenate(
-        [wide[pl.ds(rows * fac + s, n, stride=chunk), :] for s in range(rows)], axis=0
-    )
-    count[...] = mm(jnp.transpose(live_all).astype(BF16), live_all.astype(BF16))
-    for e in range(fac):
-        product = mm(left_t, right_at(e)).astype(BF16)
-        for i in range(own):
-            outer_cat[e * fac : (e + 1) * fac, i * res : (i + 1) * res] = product[i * fac : (i + 1) * fac]
+    for e in range(0, fac, 2):
+        product = mm(left_t, jnp.concatenate([right_at(e), right_at(e + 1)], axis=1)).astype(BF16)
+        for k in range(2):
+            for i in range(own):
+                outer_cat[(e + k) * fac : (e + k + 1) * fac, i * res : (i + 1) * res] = product[
+                    i * fac : (i + 1) * fac, k * res : (k + 1) * res
+                ]
     opm = mm(w_outer_t[...], outer_cat[...])
     for i in range(own):
         cols = slice(i * res, (i + 1) * res)
-        base[:, cols] = base[:, cols] + opm[:, cols] / (0.001 + count[pl.ds(me * own + i, 1), :])
+        base[:, cols] = base[:, cols] + opm[:, cols] * (1.0 / (0.001 + count[pl.ds(me * own + i, 1), :]))
     updated = base[...].astype(BF16).astype(F32)
     base[...] = updated
     pair_norm = norm_over(updated, 0).astype(BF16)
@@ -181,21 +252,21 @@
                     c * n : (c + 1) * n, k * res : (k + 1) * res
                 ]
     tri_send[...] = wide[0 : n * lines, :].astype(BF16).reshape(tri_send.shape)
-    bias_t = lax.dot_general(w_bias[...], pair_norm, OVER_FIRST, preferred_element_type=F32)
+    def send_tri(t, _):
+        to = lax.rem(me + t, n)
+        copy_to(2, t, tri_send.at[to], tri_recv.at[me]).start()
+        return 0
+
+    def send_bias(t, _):
+        copy_to(3, t, bias_send, bias_recv.at[me]).start()
+        return 0
+
+    lax.fori_loop(1, n, send_tri, 0)
+    loads[10].wait()
+    bias_t = mm(w_bias[...], pair_norm)
     bias_send[...] = jnp.concatenate(
         [bias_t[:, i * res : (i + 1) * res] for i in range(own)], axis=0
     ).astype(BF16)
-
-    def send_tri(t, _):
-        to = lax.rem(me + t, n)
-        copy_to(2, t, tri_send.at[to], tri_recv.at[me]).start()
-        return 0
-
-    def send_bias(t, _):
-        copy_to(3, t, bias_send, bias_recv.at[me]).start()
-        return 0
-
-    lax.fori_loop(1, n, send_tri, 0)
     lax.fori_loop(1, n, send_bias, 0)
     tri_recv[me] = tri_send[me]
     bias_recv[me] = bias_send[...]
@@ -203,7 +274,7 @@
 
     def wait_tri(t, _):
         frm = lax.rem(me + t, n)
-        arrived(2, t, tri_send.at[frm], tri_recv.at[frm]).wait()
+        arrived(2, t, tri_send.at[frm], tri_recv.at[frm]).wait_recv()
         return 0
 
     lax.fori_loop(1, n, wait_tri, 0)
@@ -229,9 +300,10 @@
     lax.fori_loop(1, n, send_sum, 0)
     sum_recv[me] = sum_send[me]
 
+    loads[9].wait()
     def wait_bias(t, _):
         frm = lax.rem(me + t, n)
-        arrived(3, t, bias_send, bias_recv.at[frm]).wait()
+        arrived(3, t, bias_send, bias_recv.at[frm]).wait_recv()
         return 0
 
     lax.fori_loop(1, n, wait_bias, 0)
@@ -252,14 +324,14 @@
             )
             scores = scores * scale + bias_wide[pl.ds(h, res, stride=heads), :] + mask
             scores = jnp.exp(scores - jnp.max(scores, axis=1, keepdims=True))
-            weights = (scores / jnp.sum(scores, axis=1, keepdims=True)).astype(BF16)
+            weights = (scores * (1.0 / jnp.sum(scores, axis=1, keepdims=True))).astype(BF16)
             attended = jnp.where(at_head, mm(weights, value), attended)
         gated = (gate * attended).astype(BF16)
         msa_out[s] = (msa[s].astype(F32) + mm(gated, w_final[...])).astype(BF16)
 
     def wait_sum(t, _):
         frm = lax.rem(me + t, n)
-        arrived(4, t, sum_send.at[frm], sum_recv.at[frm]).wait()
+        arrived(4, t, sum_send.at[frm], sum_recv.at[frm]).wait_recv()
         return 0
 
     lax.fori_loop(1, n, wait_sum, 0)
@@ -272,6 +344,23 @@
         cols = slice(i * res, (i + 1) * res)
         result = base[:, cols] + gating[:, cols] * mm(out_t, tri_normed)
         pair_out[i] = jnp.transpose(result).astype(BF16)
+
+    def all_sent(t, _):
+        to = lax.rem(me + t, n)
+        copy_to(1, t, left_send.at[to], left_recv.at[me]).wait_send()
+        copy_to(2, t, tri_send.at[to], tri_recv.at[me]).wait_send()
+        copy_to(3, t, bias_send, bias_recv.at[me]).wait_send()
+        copy_to(4, t, sum_send.at[to], sum_recv.at[me]).wait_send()
+        return 0
+
+    def right_sent(t, _):
+        right_out(t).wait_send()
+        right_on(t).wait_send()
+        return 0
+
+    lax.fori_loop(1, n, all_sent, 0)
+    lax.fori_loop(1, chips, right_sent, 0)
+    to_sibling.wait_send()
 
 
 def fused_on_device(
@@ -283,18 +372,23 @@
     heads = w_bias.shape[1]
     tri = w_out.shape[0]
     per = tri // n
-    chunk = rows * fac + 16
+    chunk = rows * fac
     lines = 2 * per * own
-    wide_rows = max(n * chunk, n * lines, fac * fac, rows * res, per * res)
+    wide_rows = max(n * chunk + 8 * n, n * lines, per * res)
     vmem = pl.BlockSpec(memory_space=pltpu.VMEM)
+    args = (
+        msa, live, pair, chain.reshape(1, res), number.reshape(1, res), table,
+        w_factor.T, w_outer, w_entry, w_final, w_bias.T, w_tri, w_gate, w_out,
+    )
     return pl.pallas_call(
         functools.partial(fused, n),
         out_shape=(jax.ShapeDtypeStruct(msa.shape, BF16), jax.ShapeDtypeStruct(pair.shape, BF16)),
-        in_specs=[vmem] * 14,
+        in_specs=[pl.BlockSpec(memory_space=pltpu.HBM)] * 14,
         out_specs=(vmem, vmem),
         scratch_shapes=[
-            pltpu.VMEM((n, own * rows, res), F32),
-            pltpu.VMEM((n, own * rows, res), F32),
+            *[pltpu.VMEM(a.shape, a.dtype) for a in args],
+            pltpu.VMEM((n, 8, res), LEFT),
+            pltpu.VMEM((n, 8, res), LEFT),
             pltpu.VMEM((chunk, res), BF16),
             pltpu.VMEM((n, chunk, res), BF16),
             pltpu.VMEM((n, lines, res), BF16),
@@ -311,16 +405,15 @@
             pltpu.VMEM((rows, res, 4 * feats), BF16),
             pltpu.VMEM((res, res), F32),
             pltpu.VMEM((n * own * heads, res), F32),
+            pltpu.VMEM((fac * fac, cz), F32),
             pltpu.SemaphoreType.DMA((5, n)),
             pltpu.SemaphoreType.DMA((5, n)),
+            pltpu.SemaphoreType.DMA((14,)),
         ],
         compiler_params=pltpu.CompilerParams(
-            collective_id=0, has_side_effects=True, vmem_limit_bytes=48 * 1024 * 1024
+            collective_id=0, has_side_effects=True, vmem_limit_bytes=64 * 1024 * 1024 - 4096
         ),
-    )(
-        msa, live, pair, chain.reshape(1, res), number.reshape(1, res), table,
-        w_factor, w_outer, w_entry, w_final, w_bias, w_tri, w_gate, w_out,
-    )
+    )(*args)
 
 
 def layer_normalize(values):
@@ -519,7 +612,9 @@
             res == pair.shape[2] == w_out.shape[0] == 128
             and res % n == 0
             and w_out.shape[0] % n == 0
-            and (res // n) * rows == 8
+            and n % 8 == 0
+            and rows == 2
+            and (res // n) * (blocks[6].shape[1] // 2) == res
         )
         return fused_on_device(n, *blocks) if fits else on_device(*blocks)
 

time: 57.4 us -> 42.8 us (0.75)
  local copies, waits for them, and re-layouts: 9.99 us -> 2.26 us
  Pallas kernels: 46.1 us -> 39.7 us
    unnamed x30 -> x4, local copies, waits for them, and re-layouts: 9.99 us -> 2.26 us
    pallas_call x1, Pallas kernels: 46.1 us -> 39.7 us  [fused_on_device(): pl.pallas_call(functools.partial(fused, n), out_shape=(jax.ShapeDtypeStru...]
where the time goes in v2:
time: 42.8 us; the launch traced here: 42.6 us
  Pallas kernels  39.7 us (93%)
  local copies, waits for them, and re-layouts  2.26 us (5%)
  between operations  0.65 us (2%)
    pallas_call x1, Pallas kernels, fused_on_device(): pl.pallas_call(functools.partial(fused, n), out_shape=(jax.ShapeDtypeStru...  39.7 us
    unnamed x4, local copies, waits for them, and re-layouts  2.26 us

profile of v2, /device:TPU:0, one launch (start us, length us, event | category | flops | bytes accessed | tf_op | source)
XLA Modules:
  0.0 42.6 jit_solution(7619206717005710407)
XLA Ops:
  0.6 39.7 %shard_map.149 = (bf16[2,128,256]{2,1,0:T(8,128)(2,1)}, bf16[4,128,128]{2,1,0:T(8,128)(2,1)}) custom-call(bf16[2,128,256]{2,1,0:T(8,128)(2,1)} %refs_0_.1, s32[2,128]{1,0:T(2,128)} %refs_1_.1, bf16[4,128,128]{2,1,0:T(8,128)(2,1)} %refs_2_.1, s32[1,128]{1,0:T(1,128)} %bitcast.6, s32[1,128]{1,0:T(1,128)} %bitcast.7, f32[66,128]{1,0:T(8,128)} %refs_5_.1, ...), custom_call_target="tpu_custom_call" | custom-call | tf_op jit(solution)/shard_map/pallas_call | solution.py:383
  40.3 0.0 copy-start
  40.3 1.6 %copy.18 = bf16[2,128,256]{2,1,0:T(8,128)(2,1)} copy(bf16[2,128,256]{2,1,0:T(8,128)(2,1)} %get-tuple-element.4) | data formatting | bytes 262144
  41.9 0.0 copy-done
  41.9 0.7 %copy.19 = bf16[4,128,128]{2,1,0:T(8,128)(2,1)} copy(bf16[4,128,128]{2,1,0:T(8,128)(2,1)S(1)} %copy-done) | data formatting | bytes 262144
Async XLA Ops:
  40.3 1.6 %copy-start = (bf16[4,128,128]{2,1,0:T(8,128)(2,1)S(1)}, bf16[4,128,128]{2,1,0:T(8,128)(2,1)}, u32[]{:S(2)}) copy-start(bf16[4,128,128]{2,1,0:T(8,128)(2,1)} %get-tuple-element.5) | copy-start | bytes 393220

commit v3 on v2

--- a/solution.py
+++ b/solution.py
@@ -35,7 +35,7 @@
 def fused_body(
     n, inputs, landed, msa_out, pair_out,
     left_send, left_recv, right_send, right_recv, tri_send, tri_recv, bias_send, bias_recv, sum_send, sum_recv,
-    wide, outer_cat, w_outer_t, w_tri_t, base, qkvg, count, bias_wide, outer_wide,
+    wide, outer_cat, w_outer_t, w_tri_t, base, qkvg, count, bias_wide, outer_wide, logits,
     send_sem, recv_sem, load_sem,
 ):
     msa, live_in, pair, chain, number, table, w_factor, w_outer, w_entry, w_final, w_bias, w_tri, w_gate, w_out = landed
@@ -271,6 +271,17 @@
     tri_recv[me] = tri_send[me]
     bias_recv[me] = bias_send[...]
     gating = jax.nn.sigmoid(mm(gate_t, pair_norm))
+    column = lax.broadcasted_iota(jnp.int32, (1, feats), 1)
+    scale = span ** (-0.5)
+    for s in range(rows):
+        query = qkvg[s, :, 0:feats]
+        key = qkvg[s, :, feats : 2 * feats]
+        for h in range(heads):
+            at_head = (column >= h * span) & (column < (h + 1) * span)
+            scores = lax.dot_general(
+                jnp.where(at_head, query, jnp.zeros_like(query)), key, OVER_LAST, preferred_element_type=F32
+            )
+            logits[s, h] = scores * scale
 
     def wait_tri(t, _):
         frm = lax.rem(me + t, n)
@@ -308,21 +319,14 @@
 
     lax.fori_loop(1, n, wait_bias, 0)
     bias_wide[...] = bias_recv[...].astype(F32).reshape(bias_wide.shape)
-    column = lax.broadcasted_iota(jnp.int32, (1, feats), 1)
-    scale = span ** (-0.5)
     for s in range(rows):
-        query = qkvg[s, :, 0:feats]
-        key = qkvg[s, :, feats : 2 * feats]
         value = qkvg[s, :, 2 * feats : 3 * feats]
         gate = jax.nn.sigmoid(qkvg[s, :, 3 * feats :].astype(F32))
         mask = 1000000000.0 * (live[s : s + 1, :] - 1.0)
         attended = jnp.zeros((res, feats), F32)
         for h in range(heads):
             at_head = (column >= h * span) & (column < (h + 1) * span)
-            scores = lax.dot_general(
-                jnp.where(at_head, query, jnp.zeros_like(query)), key, OVER_LAST, preferred_element_type=F32
-            )
-            scores = scores * scale + bias_wide[pl.ds(h, res, stride=heads), :] + mask
+            scores = logits[s, h] + bias_wide[pl.ds(h, res, stride=heads), :] + mask
             scores = jnp.exp(scores - jnp.max(scores, axis=1, keepdims=True))
             weights = (scores * (1.0 / jnp.sum(scores, axis=1, keepdims=True))).astype(BF16)
             attended = jnp.where(at_head, mm(weights, value), attended)
@@ -406,6 +410,7 @@
             pltpu.VMEM((res, res), F32),
             pltpu.VMEM((n * own * heads, res), F32),
             pltpu.VMEM((fac * fac, cz), F32),
+            pltpu.VMEM((rows, heads, res, res), F32),
             pltpu.SemaphoreType.DMA((5, n)),
             pltpu.SemaphoreType.DMA((5, n)),
             pltpu.SemaphoreType.DMA((14,)),

time: 42.8 us -> 42.8 us (level)
  no operation moved by 1% of the time
where the time goes in v3:
time: 42.8 us; the launch traced here: 42.6 us
  Pallas kernels  39.7 us (93%)
  local copies, waits for them, and re-layouts  2.26 us (5%)
  between operations  0.65 us (2%)
    pallas_call x1, Pallas kernels, fused_on_device(): pl.pallas_call(functools.partial(fused, n), out_shape=(jax.ShapeDtypeStru...  39.7 us
    unnamed x4, local copies, waits for them, and re-layouts  2.26 us

profile of v3, /device:TPU:0, one launch (start us, length us, event | category | flops | bytes accessed | tf_op | source)
XLA Modules:
  0.0 42.6 jit_solution(12299006997692275091)
XLA Ops:
  0.6 39.7 %shard_map.149 = (bf16[2,128,256]{2,1,0:T(8,128)(2,1)}, bf16[4,128,128]{2,1,0:T(8,128)(2,1)}) custom-call(bf16[2,128,256]{2,1,0:T(8,128)(2,1)} %refs_0_.1, s32[2,128]{1,0:T(2,128)} %refs_1_.1, bf16[4,128,128]{2,1,0:T(8,128)(2,1)} %refs_2_.1, s32[1,128]{1,0:T(1,128)} %bitcast.6, s32[1,128]{1,0:T(1,128)} %bitcast.7, f32[66,128]{1,0:T(8,128)} %refs_5_.1, ...), custom_call_target="tpu_custom_call" | custom-call | tf_op jit(solution)/shard_map/pallas_call | solution.py:387
  40.3 0.0 copy-start
  40.3 1.6 %copy.18 = bf16[2,128,256]{2,1,0:T(8,128)(2,1)} copy(bf16[2,128,256]{2,1,0:T(8,128)(2,1)} %get-tuple-element.4) | data formatting | bytes 262144
  41.9 0.0 copy-done
  41.9 0.7 %copy.19 = bf16[4,128,128]{2,1,0:T(8,128)(2,1)} copy(bf16[4,128,128]{2,1,0:T(8,128)(2,1)S(1)} %copy-done) | data formatting | bytes 262144
Async XLA Ops:
  40.3 1.6 %copy-start = (bf16[4,128,128]{2,1,0:T(8,128)(2,1)S(1)}, bf16[4,128,128]{2,1,0:T(8,128)(2,1)}, u32[]{:S(2)}) copy-start(bf16[4,128,128]{2,1,0:T(8,128)(2,1)} %get-tuple-element.5) | copy-start | bytes 393220
